TPU v7x, 256 devices: a whole 4x4x8 slice. The times are simulated.
256 devices in a mesh: blk: 64 (over y_lo, x, z), states: 4 (over y_hi, core).
Axes of the slice: x: 4, y: 4 (y_hi: 2, y_lo: 2; y = y_hi * 2 + y_lo), z: 8, core: 2. Of those that a mesh axis runs over, the one named last changes fastest.
Arguments:
- start_states: float32 [128, 16, 128, 512], P('blk', None, None, 'states'), may hold values from -6 to 6
- couplings: float32 [16, 128, 128], replicated, may hold values from -0.1875 to 0.1875
- potential: float32 [128, 16, 128], P('blk'), may hold values from -18 to 18
- site_offsets: int32 [128, 6, 16], P('blk'), may hold values from 0 to 15
- coupling_index: int32 [128, 7, 16], P('blk'), may hold values from 0 to 15
- degrees: int32 [512], P('states'), may hold values from 1 to 3, as said below
Outputs:
- orthonormal: float32 [128, 16, 128, 512], P('blk', 'states')
Inputs may be any that keep to these rules, and one draw needn't show every extreme that they name: `degrees`: every degree from 1 to 3 belongs to some state.
All inputs are finite; a program needn't handle non-finite values.
Results may differ from a plain program's by a relative error of at most 0.0003.
Values sent between devices are 32-bit elements; how exact they have to be, the bound alone decides.
A program may use at most 128 MiB of HBM per device.

v0:
```python
import jax
import jax.numpy as jnp
from jax import lax
from jax.sharding import PartitionSpec as P

cut_share = 0.3
exact = lax.Precision.HIGHEST


def padded_2(shard, sides, width):
    for axis, dim in sides:
        devices, length = (lax.axis_size(axis), shard.shape[dim])
        up = [(i, (i + 1) % devices) for i in range(devices)]
        down = [(j, i) for i, j in up]
        last = lax.slice_in_dim(shard, length - width, length, axis=dim)
        first = lax.slice_in_dim(shard, 0, width, axis=dim)
        before = lax.ppermute(last, axis, up)
        after = lax.ppermute(first, axis, down)
        shard = jnp.concatenate([before, shard, after], axis=dim)
    return shard


def copy_for_each(shard, axis):
    copies = jnp.broadcast_to(shard, (lax.axis_size(axis), *shard.shape))
    return lax.all_to_all(copies, axis, split_axis=0, concat_axis=0, tiled=True)


def folded_in_pairs(pieces, combine):
    while len(jax.tree.leaves(pieces)[0]) > 1:
        pieces = jax.vmap(combine)(
            *(jax.tree.map(lambda part: part[side::2], pieces) for side in (0, 1))
        )
    return jax.tree.map(lambda part: part[0], pieces)


def joined_all(shard, axis, combine):
    pieces = jax.tree.map(lambda part: copy_for_each(part, axis), shard)
    return folded_in_pairs(pieces, combine)


def coupling_blocks(couplings, index_rows):
    return jnp.take(couplings, index_rows, axis=0)


def apply_inner(padded, blocks_used, onsite, offset_rows):
    middle = padded[1:-1]
    lower_layers = padded[:-2]
    upper_layers = padded[2:]
    count = onsite.shape[1]
    site_ids = jnp.arange(count, dtype=jnp.int32)
    layer_ids = jnp.arange(middle.shape[0], dtype=jnp.int32)
    pieces = [middle]
    for slot in range(1, 7):
        if slot == 5:
            source = lower_layers
        elif slot == 6:
            source = upper_layers
        else:
            source = middle
        neighbour = (site_ids[None, :] + offset_rows[:, slot - 1, :]) % count
        pieces.append(source[layer_ids[:, None], neighbour])
    stacked = jnp.stack(pieces, axis=1)
    summed = jnp.einsum("lksij,lksjn->lsin", blocks_used, stacked, precision=exact)
    return summed + onsite[..., None] * middle


def extrema_of(couplings, onsite, index_rows):
    row_abs = jnp.sum(jnp.abs(couplings), axis=2)
    diag_all = jnp.diagonal(couplings, axis1=1, axis2=2)
    table_ids = jnp.arange(couplings.shape[0], dtype=jnp.int32)
    onehot = (index_rows[..., None] == table_ids).astype(jnp.float32)
    picked_abs = jnp.einsum("lksc,ci->lksi", onehot, row_abs, precision=exact)
    picked_diag = jnp.einsum("lsc,ci->lsi", onehot[:, 0], diag_all, precision=exact)
    centers = picked_diag + onsite
    radii = picked_abs[:, 0] - jnp.abs(picked_diag) + jnp.sum(picked_abs[:, 1:], axis=1)
    return (jnp.max(centers + radii), jnp.min(centers - radii))


def combine(first, second):
    return (jnp.maximum(first[0], second[0]), jnp.minimum(first[1], second[1]))


def faces(field):
    return padded_2(field, (("blk", 0),), 1)


def per_device(start_states, couplings, potential, site_offsets, coupling_index, degrees):
    upper, lower = joined_all(extrema_of(couplings, potential, coupling_index), "blk", combine)
    cut_edge = lower + cut_share * (upper - lower)
    middle_value = (upper + cut_edge) / 2.0
    half_width = (upper - cut_edge) / 2.0

    def scaled(applied, field):
        return (applied - middle_value * field) / half_width

    local_blocks = coupling_blocks(couplings, coupling_index)
    first_step = scaled(
        apply_inner(faces(start_states), local_blocks, potential, site_offsets), start_states
    )
    second = (
        2.0
        * scaled(apply_inner(faces(first_step), local_blocks, potential, site_offsets), first_step)
        - start_states
    )
    third = (
        2.0 * scaled(apply_inner(faces(second), local_blocks, potential, site_offsets), second)
        - first_step
    )
    chosen = jnp.where(degrees == 1, first_step, jnp.where(degrees == 2, second, third))
    regrouped = lax.all_to_all(chosen, "states", split_axis=1, concat_axis=3, tiled=True)
    rows = regrouped.reshape(-1, regrouped.shape[-1])
    partial_gram = lax.dot_general(
        rows, rows, (((0,), (0,)), ((), ())), precision=exact, preferred_element_type=jnp.float32
    )
    gram = lax.psum(partial_gram, ("blk", "states"))
    factor = jnp.linalg.cholesky(gram)
    identity = jnp.eye(gram.shape[0], dtype=jnp.float32)
    inverse_factor = jax.scipy.linalg.solve_triangular(factor, identity, lower=True)
    orthonormal = jnp.dot(
        rows, inverse_factor.T, precision=exact, preferred_element_type=jnp.float32
    )
    return orthonormal.reshape(regrouped.shape)


def solution(mesh):
    in_specs = (
        P("blk", None, None, "states"),
        P(),
        P("blk", None, None),
        P("blk", None, None),
        P("blk", None, None),
        P("states"),
    )
    out_specs = P("blk", "states", None, None)
    return jax.shard_map(
        per_device, mesh=mesh, in_specs=in_specs, out_specs=out_specs, check_vma=False
    )
```

profile of v0, /device:TPU:2, one launch (start us, length us, event | category | flops | bytes accessed | tf_op | source)
XLA Modules:
  0.0 722.4 jit_solution(9385407167922655574)
XLA Ops:
  8.1 6.1 copy.46
  18.6 13.0 %all-to-all-start = ((f32[64,1,1]{2,1,0:T(1,128)}), f32[64,1,1]{2,1,0:T(1,128)S(1)}, u32[]{:S(2)}, u32[]{:S(2)}) async-start(f32[64,1,1]{2,1,0:T(1,128)} %broadcast_in_dim.49), calls=%async_computation | async-start | bytes 65536 | tf_op jit(solution)/shard_map/all_to_all | solution.py:25
  33.2 2.7 collective-permute-start.1
  45.9 3.4 constant_dynamic-update-slice_fusion.5
  55.6 6.7 gather_fusion
  63.7 12.0 %all-to-all-start.1 = ((f32[64,1,1]{2,1,0:T(1,128)}), f32[64,1,1]{2,1,0:T(1,128)S(1)}, u32[]{:S(2)}, u32[]{:S(2)}) async-start(f32[64,1,1]{2,1,0:T(1,128)} %broadcast_in_dim.50), calls=%async_computation.1 | async-start | bytes 65536 | tf_op jit(solution)/shard_map/all_to_all | solution.py:25
  77.5 7.6 %all-to-all-done.1 = f32[64,1,1]{2,1,0:T(1,128)S(1)} async-done(((f32[64,1,1]{2,1,0:T(1,128)}), f32[64,1,1]{2,1,0:T(1,128)S(1)}, u32[]{:S(2)}, u32[]{:S(2)}) %all-to-all-start.1) | async-done | bytes 288 | tf_op jit(solution)/shard_map/all_to_all | solution.py:25
  90.6 4.1 pad_maximum_fusion.4
  94.7 3.6 gather_fusion.5
  98.3 3.1 constant_dynamic-update-slice_fusion.1
  101.4 3.6 gather_fusion.6
  105.0 3.1 constant_dynamic-update-slice_fusion
  108.1 21.0 %bitcast_dynamic-update-slice_fusion.2 = (f32[2,7,16,128,128]{4,3,2,0,1:T(8,128)}, f32[2,16,128,128]{3,2,1,0:T(8,128)S(1)}) fusion(f32[]{:T(128)S(6)} %div.29, f32[2,16,128,128]{3,2,1,0:T(8,128)S(1)} %copy-done.1, f32[]{:T(128)S(6)} %div.28, f32[2,16,128]{2,1,0:T(8,128)S(1)} %copy-done.22, f32[2,7,16,128,128]{4,3,1,2,0:T(8,128)} %constant_dynamic-update-slice_fusion, ...), kind=kOutput, calls=%fused_computation.56 | convolution fusion | flops 5643436032 | bytes 35668200 | tf_op jit(solution)/shard_map/lksij,lksjn->lsin/dot_general | solution.py:63
  133.6 3.6 gather_fusion.8
  137.2 3.6 gather_fusion.9
  140.8 3.6 gather_fusion.10
  144.4 3.6 gather_fusion.11
  148.0 3.3 constant_dynamic-update-slice_fusion.11
  158.3 3.6 pad_maximum_fusion.2
  161.9 3.6 gather_fusion.12
  165.5 3.6 gather_fusion.13
  169.1 3.3 constant_dynamic-update-slice_fusion.7
  173.9 21.6 %bitcast_dynamic-update-slice_fusion.1 = (f32[2,7,16,128,128]{4,3,2,0,1:T(8,128)}, f32[2,16,128,128]{3,2,1,0:T(8,128)}) fusion(f32[2,16,128,128]{3,2,1,0:T(8,128)S(1)} %copy-done.1, f32[]{:T(128)S(6)} %div.29, f32[2,16,128,128]{3,2,1,0:T(8,128)} %copy-done.2, f32[]{:T(128)S(6)} %div.28, f32[2,16,128]{2,1,0:T(8,128)S(1)} %copy-done.22, ...), kind=kOutput, calls=%fused_computation.50 | convolution fusion | flops 5644484608 | bytes 37765352 | tf_op jit(solution)/shard_map/lksij,lksjn->lsin/dot_general | solution.py:63
  195.5 2.9 fusion.105
  198.4 3.8 collective-permute-start.5
  210.5 3.3 constant_dynamic-update-slice_fusion.17
  221.8 4.3 collective-permute-done.4
  226.0 4.0 pad_maximum_fusion
  232.3 3.6 gather_fusion.19
  241.2 21.2 %fusion.19 = f32[2,16,128,128]{3,2,1,0:T(8,128)} fusion(f32[2,16,128,128]{3,2,1,0:T(8,128)S(1)} %copy-done.4, f32[2,16,128,128]{3,2,1,0:T(8,128)S(1)} %copy-done.6, f32[2,7,16,128,128]{4,3,2,0,1:T(8,128)} %constant_dynamic-update-slice_fusion.12, f32[2,7,16,128,128]{4,3,2,1,0:T(8,128)} %bitcast.190, pred[2,7,16]{1,2,0:T(8,128)(4,1)S(1)} %copy.43, ...), kind=kOutput, calls=%fused_computation.49 | convolution fusion | flops 5645533184 | bytes 35668456 | tf_op jit(solution)/shard_map/lksij,lksjn->lsin/dot_general | solution.py:63
  264.2 31.1 %all_to_all.33 = f32[2,16,128,128]{3,2,0,1:T(8,128)S(1)} all-to-all(f32[2,16,128,128]{3,2,0,1:T(8,128)S(1)} %copy.52), channel_id=1, replica_groups=mesh['blk'=64,'states'=4] {'states'}, dimensions={1} | all-to-all | bytes 4194304 | tf_op jit(solution)/shard_map/all_to_all | solution.py:110
  296.7 4.5 fusion.11
  305.6 250.9 %all-reduce.3.cloned.1.call-done = f32[512,512]{0,1:T(8,128)} async-done(((f32[512,512]{0,1:T(8,128)}), f32[512,512]{0,1:T(8,128)}) %all-reduce.3.cloned.1.call-update) | async-done | bytes 1048592 | tf_op jit(solution)/shard_map/psum | solution.py:115
  556.5 2.6 copy.55
  561.6 11.7 %cholesky.104 = f32[128,128]{1,0:T(8,128)S(1)} custom-call(f32[128,128]{1,0:T(8,128)S(1)} %cholesky.266), custom_call_target="Cholesky" | custom-call | tf_op jit(solution)/shard_map/jit(cholesky)/cholesky | solution.py:116
  573.5 9.8 %custom-call.31 = f32[1,128,128]{1,2,0:T(8,128)S(1)} custom-call(f32[1,128,128]{2,1,0:T(8,128)S(1)} %get-tuple-element.48), custom_call_target="InvertDiagBlocksLowerTriangular" | custom-call | tf_op jit(solution)/shard_map/jit(cholesky)/cholesky | solution.py:116
  585.8 11.7 %cholesky.217 = f32[128,128]{1,0:T(8,128)S(1)} custom-call(f32[128,128]{1,0:T(8,128)S(1)} %cholesky.270), custom_call_target="Cholesky" | custom-call | tf_op jit(solution)/shard_map/jit(cholesky)/cholesky | solution.py:116
  597.5 10.0 %custom-call.32 = f32[1,128,128]{1,2,0:T(8,128)S(1)} custom-call(f32[1,128,128]{2,1,0:T(8,128)S(1)} %get-tuple-element.45), custom_call_target="InvertDiagBlocksLowerTriangular" | custom-call | tf_op jit(solution)/shard_map/jit(cholesky)/cholesky | solution.py:116
  609.1 11.7 %cholesky.238 = f32[128,128]{1,0:T(8,128)S(1)} custom-call(f32[128,128]{1,0:T(8,128)S(1)} %cholesky.275), custom_call_target="Cholesky" | custom-call | tf_op jit(solution)/shard_map/jit(cholesky)/cholesky | solution.py:116
  620.8 9.8 %custom-call.33 = f32[1,128,128]{1,2,0:T(8,128)S(1)} custom-call(f32[1,128,128]{2,1,0:T(8,128)S(1)} %get-tuple-element.42), custom_call_target="InvertDiagBlocksLowerTriangular" | custom-call | tf_op jit(solution)/shard_map/jit(cholesky)/cholesky | solution.py:116
  632.1 11.7 %cholesky.255 = f32[128,128]{1,0:T(8,128)S(1)} custom-call(f32[128,128]{1,0:T(8,128)S(1)} %convolution_subtract_fusion.5), custom_call_target="Cholesky" | custom-call | tf_op jit(solution)/shard_map/jit(cholesky)/cholesky | solution.py:116
  649.7 13.9 %while.1 = (s32[]{:T(128)}, f32[512,512]{1,0:T(8,128)}, s32[4,2]{0,1:T(2,128)S(1)}, f32[4,128,128]{2,1,0:T(8,128)}, s32[]{:T(128)}) while((s32[]{:T(128)}, f32[512,512]{1,0:T(8,128)}, s32[4,2]{0,1:T(2,128)S(1)}, f32[4,128,128]{2,1,0:T(8,128)}, s32[]{:T(128)}) %tuple.46), condition=%wide.while_cond, body=%wide.while_body.sunk | while | flops 2 | bytes 132205 | solution.py:118
  650.4 2.9 bitcast_dynamic-update-slice_fusion.5
  653.9 2.9 bitcast_dynamic-update-slice_fusion.5
  657.4 2.9 bitcast_dynamic-update-slice_fusion.5
  660.9 2.8 bitcast_dynamic-update-slice_fusion.5
  663.7 40.1 %custom-call.34 = f32[4,128,128]{1,2,0:T(8,128)S(1)} custom-call(f32[4,128,128]{2,1,0:T(8,128)} %get-tuple-element.12), custom_call_target="InvertDiagBlocksLowerTriangular" | custom-call | tf_op jit(solution)/shard_map/jit(_solve_triangular)/triangular_solve | solution.py:118
  710.5 4.8 fusion.30
  (187 shorter events, 94.9 us)
Async XLA Ops:
  8.1 6.2 copy-start.23
  8.1 8.3 %copy-start.22 = (f32[2,16,128]{2,1,0:T(8,128)S(1)}, f32[2,16,128]{2,1,0:T(8,128)}, u32[]{:S(2)}) copy-start(f32[2,16,128]{2,1,0:T(8,128)} %param.8) | copy-start | bytes 49156
  8.1 23.5 %copy-start.1 = (f32[2,16,128,128]{3,2,1,0:T(8,128)S(1)}, f32[2,16,128,128]{3,2,1,0:T(8,128)}, u32[]{:S(2)}) copy-start(f32[2,16,128,128]{3,2,1,0:T(8,128)} %param.6) | copy-start | bytes 6291460
  18.6 43.8 %all-to-all-start = ((f32[64,1,1]{2,1,0:T(1,128)}), f32[64,1,1]{2,1,0:T(1,128)S(1)}, u32[]{:S(2)}, u32[]{:S(2)}) async-start(f32[64,1,1]{2,1,0:T(1,128)} %broadcast_in_dim.49), calls=%async_computation | async-start | bytes 65536 | tf_op jit(solution)/shard_map/all_to_all | solution.py:25
  33.2 57.4 %collective-permute-start.1 = (f32[1,16,128,128]{3,2,1,0:T(8,128)}, f32[1,16,128,128]{3,2,1,0:T(8,128)}, u32[]{:S(2)}, u32[]{:S(2)}) collective-permute-start(f32[1,16,128,128]{3,2,1,0:T(8,128)} %get-tuple-element.37), channel_id=1, source_target_pairs={{4,0},{8,4},{12,8},{16,12},{20,16},{24,20},{28,24},{32,28},{36,32}... | collective-permute-start | bytes 3145736 | tf_op jit(solution)/shard_map/ppermute | solution.py:18
  35.9 1.5 copy-start.24
  35.9 54.7 %collective-permute-start = (f32[1,16,128,128]{3,2,1,0:T(8,128)}, f32[1,16,128,128]{3,2,1,0:T(8,128)}, u32[]{:S(2)}, u32[]{:S(2)}) collective-permute-start(f32[1,16,128,128]{3,2,1,0:T(8,128)} %get-tuple-element.38), channel_id=1, source_target_pairs={{0,4},{4,8},{8,12},{12,16},{16,20},{20,24},{24,28},{28,32},{32,36}... | collective-permute-start | bytes 3145736 | tf_op jit(solution)/shard_map/ppermute | solution.py:17
  45.9 3.4 copy-start.8
  49.3 2.3 copy-start.9
  51.6 2.3 copy-start.10
  54.0 1.6 copy-start
  63.7 21.4 %all-to-all-start.1 = ((f32[64,1,1]{2,1,0:T(1,128)}), f32[64,1,1]{2,1,0:T(1,128)S(1)}, u32[]{:S(2)}, u32[]{:S(2)}) async-start(f32[64,1,1]{2,1,0:T(1,128)} %broadcast_in_dim.50), calls=%async_computation.1 | async-start | bytes 65536 | tf_op jit(solution)/shard_map/all_to_all | solution.py:25
  75.6 480.9 %all-reduce.3.cloned.1.call-start = ((), (), s32[]{:S(2)}) async-start(), calls=%async_computation.3 | async-start | bytes 2097152 | tf_op jit(solution)/shard_map/psum | solution.py:115
  129.2 2.0 copy-start.2
  131.2 26.2 %collective-permute-start.3 = (f32[1,16,128,128]{3,2,1,0:T(8,128)}, f32[1,16,128,128]{3,2,1,0:T(8,128)S(1)}, u32[]{:S(2)}, u32[]{:S(2)}) collective-permute-start(f32[1,16,128,128]{3,2,1,0:T(8,128)} %get-tuple-element.33), channel_id=1, source_target_pairs={{4,0},{8,4},{12,8},{16,12},{20,16},{24,20},{28,24},{32,28},{36,32}... | collective-permute-start | bytes 3145736 | tf_op jit(solution)/shard_map/ppermute | solution.py:18
  132.9 24.9 %collective-permute-start.2 = (f32[1,16,128,128]{3,2,1,0:T(8,128)}, f32[1,16,128,128]{3,2,1,0:T(8,128)}, u32[]{:S(2)}, u32[]{:S(2)}) collective-permute-start(f32[1,16,128,128]{3,2,1,0:T(8,128)} %get-tuple-element.34), channel_id=1, source_target_pairs={{0,4},{4,8},{8,12},{12,16},{16,20},{20,24},{24,28},{28,32},{32,36}... | collective-permute-start | bytes 3145736 | tf_op jit(solution)/shard_map/ppermute | solution.py:17
  148.0 3.3 copy-start.16
  151.2 2.3 copy-start.15
  153.6 2.3 copy-start.12
  155.9 2.3 copy-start.3
  169.0 3.3 copy-start.18
  195.5 6.8 copy-start.25
  195.5 6.8 copy-start.5
  198.4 23.4 %collective-permute-start.5 = (f32[1,16,128,128]{3,2,1,0:T(8,128)}, f32[1,16,128,128]{3,2,1,0:T(8,128)}, u32[]{:S(2)}, u32[]{:S(2)}) collective-permute-start(f32[1,16,128,128]{3,2,1,0:T(8,128)} %get-tuple-element.29), channel_id=1, source_target_pairs={{4,0},{8,4},{12,8},{16,12},{20,16},{24,20},{28,24},{32,28},{36,32}... | collective-permute-start | bytes 3145736 | tf_op jit(solution)/shard_map/ppermute | solution.py:18
  202.2 23.9 %collective-permute-start.4 = (f32[1,16,128,128]{3,2,1,0:T(8,128)S(1)}, f32[1,16,128,128]{3,2,1,0:T(8,128)}, u32[]{:S(2)}, u32[]{:S(2)}) collective-permute-start(f32[1,16,128,128]{3,2,1,0:T(8,128)S(1)} %get-tuple-element.30), channel_id=1, source_target_pairs={{0,4},{4,8},{8,12},{12,16},{16,20},{20,24},{24,28},{28,32},{32,36}... | collective-permute-start | bytes 3145736 | tf_op jit(solution)/shard_map/ppermute | solution.py:17
  210.5 3.3 copy-start.14
  213.8 2.3 copy-start.13
  216.1 2.3 copy-start.11
  235.9 2.3 copy-start.17
  238.2 2.3 copy-start.4
  238.2 3.0 copy-start.6
  296.7 4.5 copy-start.7
  556.5 2.6 copy-start.19
  560.6 1.0 copy-start.21
  649.7 57.0 %copy-start.20 = (f32[512,512]{1,0:T(8,128)S(1)}, f32[512,512]{1,0:T(8,128)}, u32[]{:S(2)}) copy-start(f32[512,512]{1,0:T(8,128)} %fusion.46) | copy-start | bytes 3145732
Sparse Core Ops, SparseCore 0:
  301.3 255.1 all-reduce.2
where the time goes:
time: 730 us; the launch traced here: 722 us
  waiting for transfers between devices  265 us (36%)
  local copies, waits for them, and re-layouts  148 us (20%)
  other arithmetic  138 us (19%)
  matrix products  86.3 us (12%)
  starting transfers between devices  34.2 us (5%)
  blocking collectives  31.1 us (4%)
  between operations  19.3 us (3%)
    psum x1, waiting for transfers between devices, per_device(): gram = lax.psum(partial_gram, ('blk', 'states'))  251 us
    another operation x14, other arithmetic, per_device(): factor = jnp.linalg.cholesky(gram)  78.6 us
    dot_general x3, matrix products, apply_inner(): jnp.einsum('lksij,lksjn->lsin', blocks_used, stacked, precision=exact)  63.8 us
    gather x18, local copies, waits for them, and re-layouts, apply_inner(): pieces.append(source[layer_ids[:, None], neighbour])  50.7 us
    unnamed x69, local copies, waits for them, and re-layouts  48.1 us
    another operation x3, other arithmetic, per_device(): jax.scipy.linalg.solve_triangular(factor, identity, lower=True)  41.4 us
    all_to_all x1, blocking collectives, per_device(): lax.all_to_all(chosen, 'states', split_axis=1, concat_axis=3, tiled=True)  31.1 us
    all_to_all x2, starting transfers between devices, copy_for_each(): return lax.all_to_all(copies, axis, split_axis=0, concat_axis=0, tiled=True)  25 us
  transfers between devices with their start and end apart: 9, of which 5 were waited for; matrix products, arithmetic and copies ran while one was open for 10% of the time, Pallas kernels for 0%

commit v1 on v0

--- a/solution.py
+++ b/solution.py
@@ -112,7 +112,8 @@
     partial_gram = lax.dot_general(
         rows, rows, (((0,), (0,)), ((), ())), precision=exact, preferred_element_type=jnp.float32
     )
-    gram = lax.psum(partial_gram, ("blk", "states"))
+    inner = lax.psum(partial_gram, "blk")
+    gram = lax.psum(inner, "states")
     factor = jnp.linalg.cholesky(gram)
     identity = jnp.eye(gram.shape[0], dtype=jnp.float32)
     inverse_factor = jax.scipy.linalg.solve_triangular(factor, identity, lower=True)

time: 730 us -> 1140 us (1.56)
  waiting for transfers between devices: 265 us -> 667 us
    psum x1 -> x2, waiting for transfers between devices: 251 us -> 653 us  [the longest x1 597 us: per_device(): inner = lax.psum(partial_gram, 'blk')]
    unnamed x69 -> x65, local copies, waits for them, and re-layouts: 48.1 us -> 48.4 us
  transfers between devices with their start and end apart: 9 -> 10, of which waited for: 5 -> 6; matrix products, arithmetic and copies ran while one was open for 10% -> 7% of each run, Pallas kernels for 0% -> 0%
where the time goes in v1:
time: 1140 us; the launch traced here: 1130 us
  waiting for transfers between devices  667 us (59%)
  local copies, waits for them, and re-layouts  151 us (13%)
  other arithmetic  138 us (12%)
  matrix products  86.7 us (8%)
  starting transfers between devices  34.3 us (3%)
  blocking collectives  31.1 us (3%)
  between operations  19.1 us (2%)
    psum x1, waiting for transfers between devices, per_device(): inner = lax.psum(partial_gram, 'blk')  597 us
    another operation x14, other arithmetic, per_device(): factor = jnp.linalg.cholesky(gram)  78.6 us
    dot_general x3, matrix products, apply_inner(): jnp.einsum('lksij,lksjn->lsin', blocks_used, stacked, precision=exact)  64.3 us
    psum x1, waiting for transfers between devices, per_device(): gram = lax.psum(inner, 'states')  55.9 us
    gather x18, local copies, waits for them, and re-layouts, apply_inner(): pieces.append(source[layer_ids[:, None], neighbour])  52 us
    unnamed x65, local copies, waits for them, and re-layouts  48.4 us
    another operation x3, other arithmetic, per_device(): jax.scipy.linalg.solve_triangular(factor, identity, lower=True)  41.4 us
    all_to_all x1, blocking collectives, per_device(): lax.all_to_all(chosen, 'states', split_axis=1, concat_axis=3, tiled=True)  31.1 us
  transfers between devices with their start and end apart: 10, of which 6 were waited for; matrix products, arithmetic and copies ran while one was open for 7% of the time, Pallas kernels for 0%

profile of v1, /device:TPU:2, one launch (start us, length us, event | category | flops | bytes accessed | tf_op | source)
XLA Modules:
  0.0 1128.2 jit_solution(15060743339823348759)
XLA Ops:
  8.1 6.1 copy.46
  18.6 13.0 %all-to-all-start = ((f32[64,1,1]{2,1,0:T(1,128)}), f32[64,1,1]{2,1,0:T(1,128)S(1)}, u32[]{:S(2)}, u32[]{:S(2)}) async-start(f32[64,1,1]{2,1,0:T(1,128)} %broadcast_in_dim.49), calls=%async_computation | async-start | bytes 65536 | tf_op jit(solution)/shard_map/all_to_all | solution.py:25
  45.8 3.3 constant_dynamic-update-slice_fusion.5
  55.5 6.7 gather_fusion
  63.5 12.0 %all-to-all-start.1 = ((f32[64,1,1]{2,1,0:T(1,128)}), f32[64,1,1]{2,1,0:T(1,128)S(1)}, u32[]{:S(2)}, u32[]{:S(2)}) async-start(f32[64,1,1]{2,1,0:T(1,128)} %broadcast_in_dim.50), calls=%async_computation.1 | async-start | bytes 65536 | tf_op jit(solution)/shard_map/all_to_all | solution.py:25
  77.4 7.6 all-to-all-done.1
  90.3 3.9 pad_maximum_fusion.4
  94.2 3.6 gather_fusion.5
  97.8 3.1 constant_dynamic-update-slice_fusion.1
  100.9 3.6 gather_fusion.6
  104.5 3.1 constant_dynamic-update-slice_fusion
  107.7 21.4 %bitcast_dynamic-update-slice_fusion.2 = (f32[2,7,16,128,128]{4,3,2,0,1:T(8,128)}, f32[2,16,128,128]{3,2,1,0:T(8,128)}) fusion(f32[]{:T(128)S(6)} %div.29, f32[2,16,128,128]{3,2,1,0:T(8,128)S(1)} %copy-done.1, f32[]{:T(128)S(6)} %div.28, f32[2,16,128]{2,1,0:T(8,128)S(1)} %copy-done.20, f32[2,7,16,128,128]{4,3,1,2,0:T(8,128)} %constant_dynamic-update-slice_fusion, ...), kind=kOutput, calls=%fused_computation.56 | convolution fusion | flops 5643436032 | bytes 35668200 | tf_op jit(solution)/shard_map/lksij,lksjn->lsin/dot_general | solution.py:63
  134.3 3.6 gather_fusion.8
  137.9 3.6 gather_fusion.9
  141.5 3.6 gather_fusion.10
  145.1 3.6 gather_fusion.11
  148.6 3.3 constant_dynamic-update-slice_fusion.11
  158.9 4.0 pad_maximum_fusion.2
  163.0 3.6 gather_fusion.12
  166.6 3.6 gather_fusion.13
  170.1 3.3 constant_dynamic-update-slice_fusion.7
  175.0 21.6 %bitcast_dynamic-update-slice_fusion.1 = (f32[2,7,16,128,128]{4,3,2,0,1:T(8,128)}, f32[2,16,128,128]{3,2,1,0:T(8,128)}) fusion(f32[2,16,128,128]{3,2,1,0:T(8,128)S(1)} %copy-done.1, f32[]{:T(128)S(6)} %div.29, f32[2,16,128,128]{3,2,1,0:T(8,128)} %get-tuple-element.62, f32[]{:T(128)S(6)} %div.28, f32[2,16,128]{2,1,0:T(8,128)S(1)} %copy-done.20, ...), kind=kOutput, calls=%fused_computation.50 | convolution fusion | flops 5644484608 | bytes 37765352 | tf_op jit(solution)/shard_map/lksij,lksjn->lsin/dot_general | solution.py:63
  196.6 3.2 fusion.105
  199.8 3.8 collective-permute-start.5
  211.9 3.3 constant_dynamic-update-slice_fusion.17
  223.3 4.5 collective-permute-done.4
  227.7 4.0 pad_maximum_fusion
  231.7 3.6 gather_fusion.18
  235.3 3.6 gather_fusion.19
  238.9 3.3 constant_dynamic-update-slice_fusion.13
  244.6 21.2 %fusion.19 = f32[2,16,128,128]{3,2,1,0:T(8,128)} fusion(f32[2,16,128,128]{3,2,1,0:T(8,128)S(1)} %copy-done.3, f32[2,16,128,128]{3,2,1,0:T(8,128)S(1)} %copy-done.4, f32[2,7,16,128,128]{4,3,2,0,1:T(8,128)} %constant_dynamic-update-slice_fusion.12, f32[2,7,16,128,128]{4,3,2,1,0:T(8,128)} %bitcast.190, pred[2,7,16]{1,2,0:T(8,128)(4,1)S(1)} %copy.43, ...), kind=kOutput, calls=%fused_computation.49 | convolution fusion | flops 5645533184 | bytes 35668456 | tf_op jit(solution)/shard_map/lksij,lksjn->lsin/dot_general | solution.py:63
  267.5 31.1 %all_to_all.33 = f32[2,16,128,128]{3,2,0,1:T(8,128)S(1)} all-to-all(f32[2,16,128,128]{3,2,0,1:T(8,128)S(1)} %copy.52), channel_id=1, replica_groups=mesh['blk'=64,'states'=4] {'states'}, dimensions={1} | all-to-all | bytes 4194304 | tf_op jit(solution)/shard_map/all_to_all | solution.py:110
  300.0 4.5 fusion.11
  304.6 597.3 %all-reduce.4.cloned.1.call-done = f32[512,512]{0,1:T(8,128)} async-done(((f32[512,512]{0,1:T(8,128)}), f32[512,512]{0,1:T(8,128)}) %all-reduce.4.cloned.1.call-update) | async-done | bytes 1048592 | tf_op jit(solution)/shard_map/psum | solution.py:115
  906.4 55.9 %all-reduce.6.cloned.1.call-done = f32[512,512]{0,1:T(8,128)} async-done(((f32[512,512]{0,1:T(8,128)}), f32[512,512]{0,1:T(8,128)}) %all-reduce.6.cloned.1.call-update) | async-done | bytes 1048592 | tf_op jit(solution)/shard_map/psum | solution.py:116
  967.3 11.7 %cholesky.104 = f32[128,128]{1,0:T(8,128)S(1)} custom-call(f32[128,128]{1,0:T(8,128)S(1)} %cholesky.266), custom_call_target="Cholesky" | custom-call | tf_op jit(solution)/shard_map/jit(cholesky)/cholesky | solution.py:117
  979.2 9.8 custom-call.31
  991.5 11.7 %cholesky.217 = f32[128,128]{1,0:T(8,128)S(1)} custom-call(f32[128,128]{1,0:T(8,128)S(1)} %cholesky.270), custom_call_target="Cholesky" | custom-call | tf_op jit(solution)/shard_map/jit(cholesky)/cholesky | solution.py:117
  1003.3 10.0 custom-call.32
  1014.8 11.7 %cholesky.238 = f32[128,128]{1,0:T(8,128)S(1)} custom-call(f32[128,128]{1,0:T(8,128)S(1)} %cholesky.275), custom_call_target="Cholesky" | custom-call | tf_op jit(solution)/shard_map/jit(cholesky)/cholesky | solution.py:117
  1026.6 9.8 custom-call.33
  1037.8 11.7 %cholesky.255 = f32[128,128]{1,0:T(8,128)S(1)} custom-call(f32[128,128]{1,0:T(8,128)S(1)} %convolution_subtract_fusion.5), custom_call_target="Cholesky" | custom-call | tf_op jit(solution)/shard_map/jit(cholesky)/cholesky | solution.py:117
  1055.5 14.1 %while.1 = (s32[]{:T(128)}, f32[512,512]{1,0:T(8,128)}, s32[4,2]{0,1:T(2,128)S(1)}, f32[4,128,128]{2,1,0:T(8,128)}, s32[]{:T(128)}) while((s32[]{:T(128)}, f32[512,512]{1,0:T(8,128)}, s32[4,2]{0,1:T(2,128)S(1)}, f32[4,128,128]{2,1,0:T(8,128)}, s32[]{:T(128)}) %tuple.46), condition=%wide.while_cond, body=%wide.while_body.sunk | while | flops 2 | bytes 132205 | solution.py:119
  1056.1 2.9 bitcast_dynamic-update-slice_fusion.5
  1059.7 2.9 bitcast_dynamic-update-slice_fusion.5
  1063.2 2.9 bitcast_dynamic-update-slice_fusion.5
  1069.6 40.1 %custom-call.34 = f32[4,128,128]{1,2,0:T(8,128)S(1)} custom-call(f32[4,128,128]{2,1,0:T(8,128)} %get-tuple-element.12), custom_call_target="InvertDiagBlocksLowerTriangular" | custom-call | tf_op jit(solution)/shard_map/jit(_solve_triangular)/triangular_solve | solution.py:119
  1116.4 4.8 fusion.30
  (186 shorter events, 98.6 us)
Async XLA Ops:
  8.1 6.2 copy-start.21
  8.1 8.3 copy-start.20
  8.1 23.5 %copy-start.1 = (f32[2,16,128,128]{3,2,1,0:T(8,128)S(1)}, f32[2,16,128,128]{3,2,1,0:T(8,128)}, u32[]{:S(2)}) copy-start(f32[2,16,128,128]{3,2,1,0:T(8,128)} %param.6) | copy-start | bytes 6291460
  18.6 43.7 %all-to-all-start = ((f32[64,1,1]{2,1,0:T(1,128)}), f32[64,1,1]{2,1,0:T(1,128)S(1)}, u32[]{:S(2)}, u32[]{:S(2)}) async-start(f32[64,1,1]{2,1,0:T(1,128)} %broadcast_in_dim.49), calls=%async_computation | async-start | bytes 65536 | tf_op jit(solution)/shard_map/all_to_all | solution.py:25
  33.1 57.2 %collective-permute-start.1 = (f32[1,16,128,128]{3,2,1,0:T(8,128)}, f32[1,16,128,128]{3,2,1,0:T(8,128)}, u32[]{:S(2)}, u32[]{:S(2)}) collective-permute-start(f32[1,16,128,128]{3,2,1,0:T(8,128)} %get-tuple-element.37), channel_id=1, source_target_pairs={{4,0},{8,4},{12,8},{16,12},{20,16},{24,20},{28,24},{32,28},{36,32}... | collective-permute-start | bytes 3145736 | tf_op jit(solution)/shard_map/ppermute | solution.py:18
  35.8 1.5 copy-start.22
  35.8 54.5 %collective-permute-start = (f32[1,16,128,128]{3,2,1,0:T(8,128)}, f32[1,16,128,128]{3,2,1,0:T(8,128)}, u32[]{:S(2)}, u32[]{:S(2)}) collective-permute-start(f32[1,16,128,128]{3,2,1,0:T(8,128)} %get-tuple-element.38), channel_id=1, source_target_pairs={{0,4},{4,8},{8,12},{12,16},{16,20},{20,24},{24,28},{28,32},{32,36}... | collective-permute-start | bytes 3145736 | tf_op jit(solution)/shard_map/ppermute | solution.py:17
  45.8 3.3 copy-start.6
  49.1 2.3 copy-start.7
  51.4 2.3 copy-start.8
  53.8 1.7 copy-start
  63.5 21.4 %all-to-all-start.1 = ((f32[64,1,1]{2,1,0:T(1,128)}), f32[64,1,1]{2,1,0:T(1,128)S(1)}, u32[]{:S(2)}, u32[]{:S(2)}) async-start(f32[64,1,1]{2,1,0:T(1,128)} %broadcast_in_dim.50), calls=%async_computation.1 | async-start | bytes 65536 | tf_op jit(solution)/shard_map/all_to_all | solution.py:25
  75.5 826.4 %all-reduce.4.cloned.1.call-start = ((), (), s32[]{:S(2)}) async-start(), calls=%async_computation.3 | async-start | bytes 2097152 | tf_op jit(solution)/shard_map/psum | solution.py:115
  131.9 26.2 %collective-permute-start.3 = (f32[1,16,128,128]{3,2,1,0:T(8,128)}, f32[1,16,128,128]{3,2,1,0:T(8,128)}, u32[]{:S(2)}, u32[]{:S(2)}) collective-permute-start(f32[1,16,128,128]{3,2,1,0:T(8,128)} %get-tuple-element.33), channel_id=1, source_target_pairs={{4,0},{8,4},{12,8},{16,12},{20,16},{24,20},{28,24},{32,28},{36,32}... | collective-permute-start | bytes 3145736 | tf_op jit(solution)/shard_map/ppermute | solution.py:18
  133.5 24.7 %collective-permute-start.2 = (f32[1,16,128,128]{3,2,1,0:T(8,128)S(1)}, f32[1,16,128,128]{3,2,1,0:T(8,128)}, u32[]{:S(2)}, u32[]{:S(2)}) collective-permute-start(f32[1,16,128,128]{3,2,1,0:T(8,128)S(1)} %get-tuple-element.34), channel_id=1, source_target_pairs={{0,4},{4,8},{8,12},{12,16},{16,20},{20,24},{24,28},{28,32},{32,36}... | collective-permute-start | bytes 3145736 | tf_op jit(solution)/shard_map/ppermute | solution.py:17
  148.6 3.3 copy-start.14
  151.9 2.3 copy-start.13
  154.2 2.3 copy-start.10
  156.6 2.3 copy-start.2
  170.1 3.3 copy-start.16
  196.6 7.2 copy-start.23
  196.6 7.2 copy-start.4
  199.8 23.4 %collective-permute-start.5 = (f32[1,16,128,128]{3,2,1,0:T(8,128)}, f32[1,16,128,128]{3,2,1,0:T(8,128)}, u32[]{:S(2)}, u32[]{:S(2)}) collective-permute-start(f32[1,16,128,128]{3,2,1,0:T(8,128)} %get-tuple-element.29), channel_id=1, source_target_pairs={{4,0},{8,4},{12,8},{16,12},{20,16},{24,20},{28,24},{32,28},{36,32}... | collective-permute-start | bytes 3145736 | tf_op jit(solution)/shard_map/ppermute | solution.py:18
  203.6 24.1 %collective-permute-start.4 = (f32[1,16,128,128]{3,2,1,0:T(8,128)}, f32[1,16,128,128]{3,2,1,0:T(8,128)}, u32[]{:S(2)}, u32[]{:S(2)}) collective-permute-start(f32[1,16,128,128]{3,2,1,0:T(8,128)} %get-tuple-element.30), channel_id=1, source_target_pairs={{0,4},{4,8},{8,12},{12,16},{16,20},{20,24},{24,28},{28,32},{32,36}... | collective-permute-start | bytes 3145736 | tf_op jit(solution)/shard_map/ppermute | solution.py:17
  211.9 3.3 copy-start.12
  215.2 2.3 copy-start.11
  217.6 2.3 copy-start.9
  238.9 3.3 copy-start.15
  242.2 2.3 copy-start.3
  300.0 4.5 copy-start.5
  304.6 657.7 %all-reduce.6.cloned.1.call-start = ((), (), s32[]{:S(2)}) async-start(), calls=%async_computation.4 | async-start | bytes 2097152 | tf_op jit(solution)/shard_map/psum | solution.py:116
  962.3 2.6 copy-start.17
  966.3 1.0 copy-start.19
  1055.4 57.2 %copy-start.18 = (f32[512,512]{1,0:T(8,128)S(1)}, f32[512,512]{1,0:T(8,128)}, u32[]{:S(2)}) copy-start(f32[512,512]{1,0:T(8,128)} %fusion.46) | copy-start | bytes 3145732
Sparse Core Ops, SparseCore 0:
  304.7 597.2 all-reduce.3
  904.6 57.6 all-reduce.5
